TPU v7x, 128 devices: a whole 4x4x4 slice. The times are simulated.
128 devices in a mesh: seq: 16 (over x_lo, z, core), tp: 8 (over y, x_hi).
Axes of the slice: x: 4 (x_hi: 2, x_lo: 2; x = x_hi * 2 + x_lo), y: 4, z: 4, core: 2. Of those that a mesh axis runs over, the one named last changes fastest.
Arguments:
- hidden_in: bfloat16 [6144, 3584], P('seq'), may hold values from -48 to 48
- joined_inputs: bfloat16 [6144, 8192], P('seq', 'tp'), may hold values from -64 to 64
- lengths: int32 [4], replicated, may hold values from 1 to 3072, 6144 in all
- o_weight: bfloat16 [4096, 3584], P('tp'), may hold values from -0.09375 to 0.09375
- gate_up: float32 [2, 3584, 7168], P(None, ('seq', 'tp')), may hold values from -0.09375 to 0.09375
- down_weight: bfloat16 [7168, 3584], P('tp'), may hold values from -0.0625 to 0.0625
- next_weight: bfloat16 [3584, 8192], P(None, 'tp'), may hold values from -0.09375 to 0.09375
- post_attn_gain: float32 [3584], replicated, may hold values from 0.1 to 1.9
- pre_ffw_gain: float32 [3584], replicated, may hold values from 0.1 to 1.9
- post_ffw_gain: float32 [3584], replicated, may hold values from 0.1 to 1.9
- next_gain: float32 [3584], replicated, may hold values from 0.1 to 1.9
Outputs:
- next_qkv: bfloat16 [6144, 8192], P('seq', 'tp')
Inputs may be any that keep to these rules, and one draw needn't show every extreme that they name: The lengths of 4 prompts laid end to end; they sum to 6144 and the longest is exactly 3072.
All inputs are finite; a program needn't handle non-finite values.
Results may differ from a plain program's by a relative error of at most 0.022.
Values may be sent and summed in bfloat16 or wider, within the bound.
A program may use at most 192 MiB of HBM per device.

v0:
```python
import jax
import jax.numpy as jnp
from jax import lax
from jax.sharding import PartitionSpec as P

HEADS = 16
KV_HEADS = 8
HEAD_DIM = 256


def rms_norm(values, gain):
    meansq = jnp.mean(values * values, axis=-1, keepdims=True)
    return values * lax.rsqrt(meansq + 1e-06) * gain


def local(
    hidden_in,
    joined_inputs,
    lengths,
    o_weight,
    gate_up,
    down_weight,
    next_weight,
    post_attn_gain,
    pre_ffw_gain,
    post_ffw_gain,
    next_gain,
):
    seq_count = lax.axis_size("seq")
    tp_count = lax.axis_size("tp")
    row_count = hidden_in.shape[0]
    model_width = hidden_in.shape[1]
    per_group = HEADS // KV_HEADS
    group_cols = (per_group + 2) * HEAD_DIM
    local_groups = joined_inputs.shape[1] // group_cols
    grouped = joined_inputs.reshape(row_count, local_groups, group_cols)
    queries = grouped[:, :, : per_group * HEAD_DIM].reshape(
        row_count, local_groups, per_group, HEAD_DIM
    )
    own_keys = grouped[:, :, per_group * HEAD_DIM : (per_group + 1) * HEAD_DIM]
    own_values = grouped[:, :, (per_group + 1) * HEAD_DIM :]
    keys_all, values_all = (
        lax.all_gather(own_keys, "seq", axis=0, tiled=True),
        lax.all_gather(own_values, "seq", axis=0, tiled=True),
    )
    total_rows = keys_all.shape[0]
    seq_index = lax.axis_index("seq")
    position = seq_index * row_count
    ends = jnp.cumsum(lengths)
    places = jnp.arange(total_rows, dtype=jnp.int32)
    prompt_ids = jnp.sum((places[:, None] >= ends[None, :]).astype(jnp.int32), axis=1)
    query_place = position + jnp.arange(row_count, dtype=jnp.int32)
    query_ids = lax.dynamic_slice_in_dim(prompt_ids, position, row_count, 0)
    scale = HEAD_DIM ** (-0.5)
    scores = (
        jnp.einsum("qgrd,kgd->qgrk", queries, keys_all, preferred_element_type=jnp.float32) * scale
    )
    allowed = (
        (query_ids[:, None] == prompt_ids[None, :]) & (places[None, :] <= query_place[:, None])
    )[:, None, None, :]
    scores = jnp.where(allowed, scores, -jnp.inf)
    peak = jnp.max(scores, axis=-1, keepdims=True)
    weights = jnp.where(allowed, jnp.exp(scores - peak), 0.0)
    norm_sum = jnp.sum(weights, axis=-1)
    blended = jnp.einsum(
        "qgrk,kgd->qgrd",
        weights.astype(jnp.bfloat16),
        values_all,
        preferred_element_type=jnp.float32,
    )
    blended = blended / norm_sum[..., None]
    attended = blended.astype(jnp.bfloat16).reshape(row_count, local_groups * per_group * HEAD_DIM)
    projected = jnp.dot(attended, o_weight, preferred_element_type=jnp.float32)

    def total_of(values):
        return lax.psum(values.astype(jnp.bfloat16), "tp").astype(jnp.float32)

    residual_mid = hidden_in.astype(jnp.float32) + rms_norm(total_of(projected), post_attn_gain)
    ffw_in = rms_norm(residual_mid, pre_ffw_gain).astype(jnp.bfloat16)
    server_low = gate_up.astype(jnp.bfloat16)
    stacked_rows = lax.all_gather(server_low, "seq", axis=1, tiled=True)
    local_units = lax.all_to_all(stacked_rows, "tp", split_axis=2, concat_axis=1, tiled=True)
    piece_rows = gate_up.shape[1]
    reordered = (
        ffw_in.reshape(row_count, seq_count, tp_count, piece_rows)
        .transpose(0, 2, 1, 3)
        .reshape(row_count, model_width)
    )
    gate = jnp.dot(reordered, local_units[0], preferred_element_type=jnp.float32)
    up_part = jnp.dot(reordered, local_units[1], preferred_element_type=jnp.float32)
    activated = (jax.nn.gelu(gate, approximate=True) * up_part).astype(jnp.bfloat16)
    ffw_out = jnp.dot(activated, down_weight, preferred_element_type=jnp.float32)
    residual_out = residual_mid + rms_norm(total_of(ffw_out), post_ffw_gain)
    next_in = rms_norm(residual_out, next_gain).astype(jnp.bfloat16)
    return jnp.dot(next_in, next_weight, preferred_element_type=jnp.float32).astype(jnp.bfloat16)


def solution(mesh):
    in_specs = (
        P("seq", None),
        P("seq", "tp"),
        P(),
        P("tp", None),
        P(None, ("seq", "tp"), None),
        P("tp", None),
        P(None, "tp"),
        P(),
        P(),
        P(),
        P(),
    )
    out_specs = P("seq", "tp")
    return jax.shard_map(local, mesh=mesh, in_specs=in_specs, out_specs=out_specs, check_vma=False)
```

profile of v0, /device:TPU:1, one launch (start us, length us, event | category | flops | bytes accessed | tf_op | source)
XLA Modules:
  0.0 658.8 jit_solution(18442453555862474000)
XLA Ops:
  6.5 0.0 all-gather.8.cloned.1.call-start
  6.5 2.9 convert_element_type.50
  9.4 0.0 all-gather.8.cloned.1.call-update
  9.4 0.0 all-gather.4.cloned.1.call-start
  9.5 1.8 fusion.53
  11.3 0.0 all-gather.4.cloned.1.call-update
  11.3 0.0 all-gather.6.cloned.1.call-start
  11.4 0.7 all-gather.6.cloned.1.call-update
  12.1 1.0 slice.23
  13.1 0.8 reduce-window.8
  13.9 0.2 copy.49
  14.1 0.1 convert_reduce_fusion
  14.3 0.1 dynamic_slice.3
  14.4 72.0 %all-gather.8.cloned.1.call-done = bf16[2,448,7168]{2,0,1:T(2,128)(2,1)} async-done(((bf16[2,28,7168]{2,0,1:T(2,128)(2,1)}), bf16[2,448,7168]{2,0,1:T(2,128)(2,1)}) %all-gather.8.cloned.1.call-update) | async-done | bytes 12845072 | tf_op jit(solution)/shard_map/all_gather | solution.py:81
  86.4 48.5 %copy.55 = bf16[2,448,7168]{1,0,2:T(2,128)(2,1)} copy(bf16[2,448,7168]{2,0,1:T(2,128)(2,1)} %all-gather.8.cloned.1.call-done) | data formatting | bytes 25690112 | tf_op jit(solution)/shard_map/all_gather | solution.py:81
  134.9 6.5 all-to-all-start
  141.4 0.0 all-reduce.3.cloned.1.call-start
  141.5 3.8 fusion.6
  145.2 0.0 all-gather.4.cloned.1.call-done
  145.2 5.4 fusion
  150.7 0.0 copy-start.2
  150.7 6.5 copy-done.2
  157.2 6.1 fusion.1
  163.3 4.7 all-gather.6.cloned.1.call-done
  167.9 0.0 copy-start.4
  167.9 13.2 %fusion.39 = bf16[1,256,384,2]{2,1,3,0:T(8,128)(2,1)S(1)} fusion(bf16[6144,1,256]{2,0,1:T(8,128)(2,1)} %all-gather.6.cloned.1.call-done, f32[6144,384,2]{1,0,2:T(8,128)} %copy-done.2, f32[384,2]{0,1:T(2,128)S(1)} %get-tuple-element.9, pred[384,6144]{0,1:T(8,128)(4,1)} %fusion.6, f32[384,2]{0,1:T(2,128)S(1)} %fusion.1), kind=kOutput, calls=%fused_computation.45 | convolution fusion | flops 2439905280 | bytes 24778752 | tf_op jit(solution)/shard_map/qgrk,kgd->qgrd/dot_general | solution.py:65
  181.1 0.0 copy-done.4
  181.1 0.0 copy-start.5
  181.2 3.2 convolution_convert_fusion
  184.3 0.0 copy-start.6
  184.3 0.0 all-reduce.3.cloned.1.call-update
  184.4 0.2 all-reduce.5.cloned.1.call-start
  184.6 232.3 %all-reduce.3.cloned.1.call-done = bf16[384,3584]{1,0:T(8,128)(2,1)} async-done(((bf16[384,3584]{1,0:T(8,128)(2,1)}), bf16[384,3584]{1,0:T(8,128)(2,1)}) %all-reduce.3.cloned.1.call-update) | async-done | bytes 2752528 | tf_op jit(solution)/shard_map/psum | solution.py:76
  416.9 0.0 copy-start
  416.9 2.5 fusion.8
  419.5 0.0 copy-done.5
  419.5 4.0 multiply_reduce_fusion.1
  423.5 0.0 copy-done.6
  423.5 0.0 copy-done
  423.5 5.1 multiply_convert_fusion.1
  428.7 4.5 copy.53
  433.2 5.2 reshape.159
  438.4 4.0 copy.54
  442.4 5.2 reshape.160
  447.6 0.0 all-to-all-done
  447.6 24.5 %copy.63 = bf16[2,448,8,896]{3,2,1,0:T(8,128)(2,1)} copy(bf16[2,448,8,896]{1,0,3,2:T(2,128)(2,1)} %bitcast.16) | data formatting | bytes 25690112 | tf_op jit(solution)/shard_map/all_to_all | solution.py:82
  472.1 8.3 %fusion.52 = (bf16[1,8,448,896]{3,1,2,0:T(8,128)(2,1)}, bf16[1,8,448,896]{3,1,2,0:T(8,128)(2,1)S(1)}) fusion(bf16[2,8,448,896]{3,1,2,0:T(8,128)(2,1)} %bitcast.80), kind=kLoop, calls=%fused_computation.60 | loop fusion | bytes 25690112 | tf_op jit(solution)/shard_map/slice | solution.py:89
  480.4 3.9 copy.57
  484.3 3.8 copy.58
  488.1 5.9 fusion.54
  494.0 13.5 %convolution_convert_fusion.1 = bf16[384,3584]{1,0:T(8,128)(2,1)} fusion(bf16[896,3584]{1,0:T(8,128)(2,1)} %param.16, bf16[384,3584]{0,1:T(8,128)(2,1)} %reshape.160, bf16[3584,896]{1,0:T(8,128)(2,1)} %bitcast.83, f32[384,896]{1,0:T(8,128)} %fusion.54), kind=kOutput, calls=%fused_computation.15 | convolution fusion | flops 4937318400 | bytes 19726336 | tf_op jit(solution)/shard_map/dot_general | solution.py:92
  507.4 0.0 copy-start.7
  507.4 0.0 all-reduce.5.cloned.1.call-update
  507.5 0.0 copy-start.8
  507.5 129.4 %all-reduce.5.cloned.1.call-done = bf16[384,3584]{1,0:T(8,128)(2,1)} async-done(((bf16[384,3584]{1,0:T(8,128)(2,1)}), bf16[384,3584]{1,0:T(8,128)(2,1)}) %all-reduce.5.cloned.1.call-update) | async-done | bytes 2752528 | tf_op jit(solution)/shard_map/psum | solution.py:76
  636.9 0.0 copy-start.1
  636.9 0.0 copy-start.3
  636.9 2.5 fusion.11
  639.5 0.0 copy-done.7
  639.5 4.8 multiply_reduce_fusion
  644.3 0.0 copy-done.8
  644.3 0.0 copy-done.1
  644.3 0.0 copy-done.3
  644.3 8.0 %fusion.20 = bf16[384,1024]{1,0:T(8,128)(2,1)} fusion(bf16[3584,1024]{1,0:T(8,128)(2,1)} %param.17, f32[3584]{0:T(1024)S(1)} %copy-done.8, f32[384]{0:T(512)S(1)} %add_rsqrt_fusion, bf16[384,3584]{1,0:T(8,128)(2,1)S(1)} %copy-done.3, bf16[384,3584]{1,0:T(8,128)(2,1)S(1)} %copy-done, bf16[384,3584]{1,0:T(8,128)(2,1)S(1)} %copy-done.1, ...), kind=kOutput, calls=%fused_computation.34 | convolution fusion | flops 2835480576 | bytes 16431616 | tf_op jit(solution)/shard_map/dot_general | solution.py:95
  (5 shorter events, 0.0 us)
Async XLA Ops:
  6.5 79.8 %all-gather.8.cloned.1.call-start = ((), (), s32[]{:S(2)}) async-start(), calls=%async_computation.4 | async-start | bytes 13647872 | tf_op jit(solution)/shard_map/all_gather | solution.py:81
  9.4 135.8 %all-gather.4.cloned.1.call-start = ((), (), s32[]{:S(2)}) async-start(), calls=%async_computation.1 | async-start | bytes 3342336 | tf_op jit(solution)/shard_map/all_gather | solution.py:43
  11.3 156.6 %all-gather.6.cloned.1.call-start = ((), (), s32[]{:S(2)}) async-start(), calls=%async_computation.2 | async-start | bytes 3342336 | tf_op jit(solution)/shard_map/all_gather | solution.py:44
  134.9 312.7 %all-to-all-start = ((bf16[2,448,7168]{1,0,2:T(2,128)(2,1)}), bf16[2,448,7168]{1,0,2:T(2,128)(2,1)}, u32[]{:S(2)}, u32[]{:S(2)}) async-start(bf16[2,448,7168]{1,0,2:T(2,128)(2,1)} %copy.55), calls=%async_computation | async-start | bytes 29360128 | tf_op jit(solution)/shard_map/all_to_all | solution.py:82
  141.4 275.5 %all-reduce.3.cloned.1.call-start = ((), (), s32[]{:S(2)}) async-start(), calls=%async_computation.3 | async-start | bytes 5505024 | tf_op jit(solution)/shard_map/psum | solution.py:76
  150.7 6.5 copy-start.2
  167.9 13.2 %copy-start.4 = (bf16[512,3584]{1,0:T(8,128)(2,1)S(1)}, bf16[512,3584]{1,0:T(8,128)(2,1)}, u32[]{:S(2)}) copy-start(bf16[512,3584]{1,0:T(8,128)(2,1)} %param.14) | copy-start | bytes 11010052
  181.1 238.4 %copy-start.5 = (f32[3584]{0:T(1024)S(1)}, f32[3584]{0:T(1024)}, u32[]{:S(2)}) copy-start(f32[3584]{0:T(1024)} %param.18) | copy-start | bytes 43012
  184.3 239.2 %copy-start.6 = (f32[3584]{0:T(1024)S(1)}, f32[3584]{0:T(1024)}, u32[]{:S(2)}) copy-start(f32[3584]{0:T(1024)} %param.19) | copy-start | bytes 43012
  184.4 452.5 %all-reduce.5.cloned.1.call-start = ((), (), s32[]{:S(2)}) async-start(), calls=%async_computation.5 | async-start | bytes 5505024 | tf_op jit(solution)/shard_map/psum | solution.py:76
  416.9 6.6 copy-start
  507.4 132.0 %copy-start.7 = (f32[3584]{0:T(1024)S(1)}, f32[3584]{0:T(1024)}, u32[]{:S(2)}) copy-start(f32[3584]{0:T(1024)} %param.20) | copy-start | bytes 43012
  507.5 136.8 %copy-start.8 = (f32[3584]{0:T(1024)S(1)}, f32[3584]{0:T(1024)}, u32[]{:S(2)}) copy-start(f32[3584]{0:T(1024)} %param.21) | copy-start | bytes 43012
  636.9 7.4 %copy-start.1 = (bf16[384,3584]{1,0:T(8,128)(2,1)S(1)}, bf16[384,3584]{1,0:T(8,128)(2,1)}, u32[]{:S(2)}) copy-start(bf16[384,3584]{1,0:T(8,128)(2,1)} %param.11) | copy-start | bytes 8257540
  636.9 7.4 %copy-start.3 = (bf16[384,3584]{1,0:T(8,128)(2,1)S(1)}, bf16[384,3584]{1,0:T(8,128)(2,1)}, u32[]{:S(2)}) copy-start(bf16[384,3584]{1,0:T(8,128)(2,1)} %all-reduce.5.cloned.1.call-done) | copy-start | bytes 8257540
Sparse Core Ops, SparseCore 0:
  9.6 76.7 all-gather.7
  88.1 37.0 all-gather.3
  126.8 41.0 all-gather.5
  184.5 232.4 all-reduce.2
  507.6 129.2 all-reduce.4
where the time goes:
time: 662 us; the launch traced here: 659 us
  waiting for transfers between devices  439 us (66%)
  local copies, waits for them, and re-layouts  118 us (18%)
  matrix products  49.1 us (7%)
  other arithmetic  32.8 us (5%)
  between operations  13.3 us (2%)
  starting transfers between devices  6.85 us (1%)
    psum x2, waiting for transfers between devices, total_of(): return lax.psum(values.astype(jnp.bfloat16), 'tp').astype(jnp.float32)  362 us
    all_gather x1, waiting for transfers between devices, local(): stacked_rows = lax.all_gather(server_low, 'seq', axis=1, tiled=True)  72 us
    all_gather x1, local copies, waits for them, and re-layouts, local(): stacked_rows = lax.all_gather(server_low, 'seq', axis=1, tiled=True)  48.5 us
    all_to_all x1, local copies, waits for them, and re-layouts, local(): lax.all_to_all(stacked_rows, 'tp', split_axis=2, concat_axis=1, tiled=True)  24.5 us
    reduce_sum x4, other arithmetic, rms_norm(): meansq = jnp.mean(values * values, axis=-1, keepdims=True)  13.9 us
    dot_general x1, matrix products, local(): jnp.dot(activated, down_weight, preferred_element_type=jnp.float32)  13.5 us
  transfers between devices with their start and end apart: 6, of which 4 were waited for; matrix products, arithmetic and copies ran while one was open for 17% of the time, Pallas kernels for 0%

commit v1 on v0

--- a/solution.py
+++ b/solution.py
@@ -79,7 +79,13 @@
     ffw_in = rms_norm(residual_mid, pre_ffw_gain).astype(jnp.bfloat16)
     server_low = gate_up.astype(jnp.bfloat16)
     stacked_rows = lax.all_gather(server_low, "seq", axis=1, tiled=True)
-    local_units = lax.all_to_all(stacked_rows, "tp", split_axis=2, concat_axis=1, tiled=True)
+    time_samples_now = lambda inp, axis_name: jnp.concatenate(
+        jax.lax.all_to_all(
+            jnp.stack(jnp.split(inp, jax.lax.axis_size(axis_name), 2)), axis_name, 0, 0
+        ),
+        1,
+    )
+    local_units = time_samples_now(stacked_rows, "tp")
     piece_rows = gate_up.shape[1]
     reordered = (
         ffw_in.reshape(row_count, seq_count, tp_count, piece_rows)

time: 662 us -> 601 us (0.908); the launches traced: 659 us -> 591 us
  local copies, waits for them, and re-layouts: 118 us -> 65.9 us
  waiting for transfers between devices: 439 us -> 414 us
  starting transfers between devices: 6.85 us -> 17.1 us
    all_gather x1 -> x0, local copies, waits for them, and re-layouts: 48.5 us -> none  [local(): stacked_rows = lax.all_gather(server_low, 'seq', axis=1, tiled=True)]
    psum x2, waiting for transfers between devices: 362 us -> 325 us  [total_of(): return lax.psum(values.astype(jnp.bfloat16), 'tp').astype(jnp.float32)]
    unnamed x18 -> x27, local copies, waits for them, and re-layouts: 6.5 us -> 25.2 us
    all_to_all x1, local copies, waits for them, and re-layouts: 24.5 us -> 6.7 us  [local(): jax.lax.all_to_all(jnp.stack(jnp.split(inp, jax.lax.axis_size(axis_name),...]
    all_gather x1, waiting for transfers between devices: 4.66 us -> 16.6 us  [local(): lax.all_gather(own_values, 'seq', axis=0, tiled=True)]
    psum x2, starting transfers between devices: 0.26 us -> 10.6 us  [total_of(): return lax.psum(values.astype(jnp.bfloat16), 'tp').astype(jnp.float32)]
    slice x2 -> x1, local copies, waits for them, and re-layouts: 12.2 us -> 3.42 us  [local(): local_units[0]]
    another operation x0 -> x2, local copies, waits for them, and re-layouts: none -> 8.46 us  [local(): jnp.stack(jnp.split(inp, jax.lax.axis_size(axis_name), 2))]
  transfers between devices with their start and end apart: 6 -> 6, of which waited for: 4 -> 4; matrix products, arithmetic and copies ran while one was open for 17% -> 16% of each run, Pallas kernels for 0% -> 0%
where the time goes in v1:
time: 601 us; the launch traced here: 591 us
  waiting for transfers between devices  414 us (69%)
  local copies, waits for them, and re-layouts  65.9 us (11%)
  matrix products  47.2 us (8%)
  other arithmetic  32.9 us (5%)
  starting transfers between devices  17.1 us (3%)
  between operations  13.7 us (2%)
    psum x2, waiting for transfers between devices, total_of(): return lax.psum(values.astype(jnp.bfloat16), 'tp').astype(jnp.float32)  325 us
    all_gather x1, waiting for transfers between devices, local(): stacked_rows = lax.all_gather(server_low, 'seq', axis=1, tiled=True)  72 us
    unnamed x27, local copies, waits for them, and re-layouts  25.2 us
    all_gather x1, waiting for transfers between devices, local(): lax.all_gather(own_values, 'seq', axis=0, tiled=True)  16.6 us
    reduce_sum x4, other arithmetic, rms_norm(): meansq = jnp.mean(values * values, axis=-1, keepdims=True)  13.9 us
    dot_general x1, matrix products, local(): jnp.dot(activated, down_weight, preferred_element_type=jnp.float32)  13.4 us
    dot_general x1, matrix products, local(): jnp.einsum('qgrk,kgd->qgrd', weights.astype(jnp.bfloat16), values_all, pr...  13.2 us
  transfers between devices with their start and end apart: 6, of which 4 were waited for; matrix products, arithmetic and copies ran while one was open for 16% of the time, Pallas kernels for 0%

profile of v1, /device:TPU:1, one launch (start us, length us, event | category | flops | bytes accessed | tf_op | source)
XLA Modules:
  0.0 591.1 jit_solution(2048562144768185990)
XLA Ops:
  6.5 0.0 all-gather.8.cloned.1.call-start
  6.5 2.9 convert_element_type.50
  9.4 0.0 all-gather.8.cloned.1.call-update
  9.4 0.0 all-gather.4.cloned.1.call-start
  9.5 1.8 fusion.61
  11.3 0.0 all-gather.4.cloned.1.call-update
  11.3 0.0 all-gather.6.cloned.1.call-start
  11.4 0.7 all-gather.6.cloned.1.call-update
  12.1 1.0 slice.23
  13.1 0.8 reduce-window.8
  13.9 0.1 convert_reduce_fusion
  14.1 0.2 copy.36
  14.3 0.1 dynamic_slice.3
  14.4 72.0 %all-gather.8.cloned.1.call-done = bf16[2,448,7168]{2,0,1:T(2,128)(2,1)} async-done(((bf16[2,28,7168]{2,0,1:T(2,128)(2,1)}), bf16[2,448,7168]{2,0,1:T(2,128)(2,1)}) %all-gather.8.cloned.1.call-update) | async-done | bytes 12845072 | tf_op jit(solution)/shard_map/all_gather | solution.py:81
  86.4 2.5 fusion.27
  88.9 2.7 fusion.26
  91.6 2.7 fusion.25
  94.3 2.7 fusion.24
  96.9 2.8 fusion.23
  99.7 2.7 fusion.22
  102.4 2.7 fusion.21
  105.1 2.7 fusion.20
  107.8 5.8 copy.42
  113.6 6.3 %all-to-all-start = ((bf16[8,2,448,896]{3,2,1,0:T(8,128)(2,1)}), bf16[8,2,448,896]{3,2,1,0:T(8,128)(2,1)}, u32[]{:S(2)}, u32[]{:S(2)}) async-start(bf16[8,2,448,896]{3,2,1,0:T(8,128)(2,1)} %copy.42), calls=%async_computation | async-start | bytes 25690112 | tf_op jit(solution)/shard_map/all_to_all | solution.py:83
  119.9 10.6 %all-reduce.3.cloned.1.call-start = ((), (), s32[]{:S(2)}) async-start(), calls=%async_computation.3 | async-start | bytes 5505024 | tf_op jit(solution)/shard_map/psum | solution.py:76
  130.5 3.8 fusion.6
  134.4 5.4 fusion
  139.8 0.0 copy-start.3
  139.8 6.5 %copy-done.3 = f32[6144,384,2]{1,0,2:T(8,128)} copy-done((f32[6144,384,2]{1,0,2:T(8,128)}, f32[6144,384,2]{1,0,2:T(8,128)S(1)}, u32[]{:S(2)}) %copy-start.3) | copy-done | bytes 18874392
  146.3 6.1 %fusion.1 = f32[384,2]{0,1:T(2,128)S(1)} fusion(f32[6144,384,2]{1,0,2:T(8,128)S(1)} %get-tuple-element.10, f32[384,2]{0,1:T(2,128)S(1)} %get-tuple-element.9, pred[384,6144]{0,1:T(8,128)(4,1)} %fusion.6), kind=kLoop, calls=%fused_computation.3 | loop fusion | flops 23592192 | bytes 21239808 | tf_op jit(solution)/shard_map/reduce_sum | solution.py:64
  152.4 16.6 %all-gather.6.cloned.1.call-done = bf16[6144,1,256]{2,0,1:T(8,128)(2,1)} async-done(((bf16[384,1,256]{2,0,1:T(8,128)(2,1)}), bf16[6144,1,256]{2,0,1:T(8,128)(2,1)}) %all-gather.6.cloned.1.call-update) | async-done | bytes 3145744 | tf_op jit(solution)/shard_map/all_gather | solution.py:44
  169.0 13.2 %fusion.47 = bf16[1,256,384,2]{2,1,3,0:T(8,128)(2,1)S(1)} fusion(bf16[6144,1,256]{2,0,1:T(8,128)(2,1)} %all-gather.6.cloned.1.call-done, f32[6144,384,2]{1,0,2:T(8,128)} %copy-done.3, f32[384,2]{0,1:T(2,128)S(1)} %get-tuple-element.9, pred[384,6144]{0,1:T(8,128)(4,1)} %fusion.6, f32[384,2]{0,1:T(2,128)S(1)} %fusion.1), kind=kOutput, calls=%fused_computation.62 | convolution fusion | flops 2439905280 | bytes 24778752 | tf_op jit(solution)/shard_map/qgrk,kgd->qgrd/dot_general | solution.py:65
  182.2 0.0 copy-done.5
  182.2 0.0 copy-start.6
  182.2 3.2 convolution_convert_fusion
  185.4 0.0 all-reduce.3.cloned.1.call-update
  185.4 0.0 all-reduce.5.cloned.1.call-start
  185.5 196.7 %all-reduce.3.cloned.1.call-done = bf16[384,3584]{1,0:T(8,128)(2,1)} async-done(((bf16[384,3584]{1,0:T(8,128)(2,1)}), bf16[384,3584]{1,0:T(8,128)(2,1)}) %all-reduce.3.cloned.1.call-update) | async-done | bytes 2752528 | tf_op jit(solution)/shard_map/psum | solution.py:76
  382.2 2.5 fusion.8
  384.7 0.0 copy-done.6
  384.7 4.0 multiply_reduce_fusion.1
  388.7 0.0 copy-done.7
  388.7 0.0 copy-done
  388.7 5.1 multiply_convert_fusion.1
  393.9 4.5 copy.40
  398.4 5.2 reshape.163
  403.6 4.0 copy.41
  407.6 5.2 reshape.164
  412.8 0.0 all-to-all-done
  412.8 6.7 %copy.49 = bf16[8,2,448,896]{3,2,0,1:T(8,128)(2,1)S(1)} copy(bf16[8,2,448,896]{3,2,1,0:T(8,128)(2,1)} %all-to-all-done) | data formatting | bytes 25690112 | tf_op jit(solution)/shard_map/all_to_all | solution.py:83
  419.5 0.0 copy-start.2
  419.6 3.4 fusion.60
  423.0 0.0 copy-done.2
  423.0 4.2 fusion.62
  427.1 13.4 %convolution_convert_fusion.1 = bf16[384,3584]{1,0:T(8,128)(2,1)} fusion(bf16[896,3584]{1,0:T(8,128)(2,1)} %param.16, bf16[384,3584]{0,1:T(8,128)(2,1)} %reshape.164, bf16[3584,896]{1,0:T(8,128)(2,1)} %bitcast.116, f32[384,896]{1,0:T(8,128)} %fusion.62), kind=kOutput, calls=%fused_computation.16 | convolution fusion | flops 4937318400 | bytes 19726336 | tf_op jit(solution)/shard_map/dot_general | solution.py:98
  440.5 0.0 all-reduce.5.cloned.1.call-update
  440.5 0.0 copy-start.9
  440.5 128.3 %all-reduce.5.cloned.1.call-done = bf16[384,3584]{1,0:T(8,128)(2,1)} async-done(((bf16[384,3584]{1,0:T(8,128)(2,1)}), bf16[384,3584]{1,0:T(8,128)(2,1)}) %all-reduce.5.cloned.1.call-update) | async-done | bytes 2752528 | tf_op jit(solution)/shard_map/psum | solution.py:76
  568.8 2.5 fusion.11
  571.4 0.0 copy-done.8
  571.4 4.8 multiply_reduce_fusion
  576.2 0.0 copy-done.9
  576.2 0.0 copy-done.1
  576.2 8.0 %fusion.28 = bf16[384,1024]{1,0:T(8,128)(2,1)} fusion(bf16[3584,1024]{1,0:T(8,128)(2,1)} %param.17, f32[3584]{0:T(1024)S(1)} %copy-done.9, f32[384]{0:T(512)S(1)} %add_rsqrt_fusion, bf16[384,3584]{1,0:T(8,128)(2,1)S(1)} %copy-done.4, bf16[384,3584]{1,0:T(8,128)(2,1)S(1)} %copy-done, bf16[384,3584]{1,0:T(8,128)(2,1)S(1)} %copy-done.1, ...), kind=kOutput, calls=%fused_computation.51 | convolution fusion | flops 2835480576 | bytes 16431616 | tf_op jit(solution)/shard_map/dot_general | solution.py:101
  (13 shorter events, 0.1 us)
Async XLA Ops:
  6.5 79.8 %all-gather.8.cloned.1.call-start = ((), (), s32[]{:S(2)}) async-start(), calls=%async_computation.4 | async-start | bytes 13647872 | tf_op jit(solution)/shard_map/all_gather | solution.py:81
  9.4 124.9 %all-gather.4.cloned.1.call-start = ((), (), s32[]{:S(2)}) async-start(), calls=%async_computation.1 | async-start | bytes 3342336 | tf_op jit(solution)/shard_map/all_gather | solution.py:43
  11.3 157.7 %all-gather.6.cloned.1.call-start = ((), (), s32[]{:S(2)}) async-start(), calls=%async_computation.2 | async-start | bytes 3342336 | tf_op jit(solution)/shard_map/all_gather | solution.py:44
  113.6 299.2 %all-to-all-start = ((bf16[8,2,448,896]{3,2,1,0:T(8,128)(2,1)}), bf16[8,2,448,896]{3,2,1,0:T(8,128)(2,1)}, u32[]{:S(2)}, u32[]{:S(2)}) async-start(bf16[8,2,448,896]{3,2,1,0:T(8,128)(2,1)} %copy.42), calls=%async_computation | async-start | bytes 25690112 | tf_op jit(solution)/shard_map/all_to_all | solution.py:83
  119.9 262.2 %all-reduce.3.cloned.1.call-start = ((), (), s32[]{:S(2)}) async-start(), calls=%async_computation.3 | async-start | bytes 5505024 | tf_op jit(solution)/shard_map/psum | solution.py:76
  139.8 6.5 %copy-start.3 = (f32[6144,384,2]{1,0,2:T(8,128)}, f32[6144,384,2]{1,0,2:T(8,128)S(1)}, u32[]{:S(2)}) copy-start(f32[6144,384,2]{1,0,2:T(8,128)S(1)} %get-tuple-element.10) | copy-start | bytes 56623108
  169.0 13.2 %copy-start.5 = (bf16[512,3584]{1,0:T(8,128)(2,1)S(1)}, bf16[512,3584]{1,0:T(8,128)(2,1)}, u32[]{:S(2)}) copy-start(bf16[512,3584]{1,0:T(8,128)(2,1)} %param.14) | copy-start | bytes 11010052
  182.2 202.5 %copy-start.6 = (f32[3584]{0:T(1024)S(1)}, f32[3584]{0:T(1024)}, u32[]{:S(2)}) copy-start(f32[3584]{0:T(1024)} %param.18) | copy-start | bytes 43012
  185.4 203.3 %copy-start.7 = (f32[3584]{0:T(1024)S(1)}, f32[3584]{0:T(1024)}, u32[]{:S(2)}) copy-start(f32[3584]{0:T(1024)} %param.19) | copy-start | bytes 43012
  185.4 383.4 %all-reduce.5.cloned.1.call-start = ((), (), s32[]{:S(2)}) async-start(), calls=%async_computation.5 | async-start | bytes 5505024 | tf_op jit(solution)/shard_map/psum | solution.py:76
  382.1 6.6 %copy-start = (bf16[384,3584]{1,0:T(8,128)(2,1)S(1)}, bf16[384,3584]{1,0:T(8,128)(2,1)}, u32[]{:S(2)}) copy-start(bf16[384,3584]{1,0:T(8,128)(2,1)} %all-reduce.3.cloned.1.call-done) | copy-start | bytes 8257540
  419.5 3.4 copy-start.2
  440.5 130.9 %copy-start.8 = (f32[3584]{0:T(1024)S(1)}, f32[3584]{0:T(1024)}, u32[]{:S(2)}) copy-start(f32[3584]{0:T(1024)} %param.20) | copy-start | bytes 43012
  440.5 135.6 %copy-start.9 = (f32[3584]{0:T(1024)S(1)}, f32[3584]{0:T(1024)}, u32[]{:S(2)}) copy-start(f32[3584]{0:T(1024)} %param.21) | copy-start | bytes 43012
  568.8 7.4 %copy-start.1 = (bf16[384,3584]{1,0:T(8,128)(2,1)S(1)}, bf16[384,3584]{1,0:T(8,128)(2,1)}, u32[]{:S(2)}) copy-start(bf16[384,3584]{1,0:T(8,128)(2,1)} %param.11) | copy-start | bytes 8257540
  568.8 7.4 %copy-start.4 = (bf16[384,3584]{1,0:T(8,128)(2,1)S(1)}, bf16[384,3584]{1,0:T(8,128)(2,1)}, u32[]{:S(2)}) copy-start(bf16[384,3584]{1,0:T(8,128)(2,1)} %all-reduce.5.cloned.1.call-done) | copy-start | bytes 8257540
Sparse Core Ops, SparseCore 0:
  9.6 76.7 all-gather.7
  88.1 38.4 all-gather.3
  128.3 40.6 all-gather.5
  185.5 196.5 all-reduce.2
  440.6 128.1 all-reduce.4
